TPU v7x, 32 devices: a whole 2x2x4 slice. The times are simulated.
32 devices in a mesh: cuts: 2 (over x), frame: 8 (over z, y), coil: 2 (over core).
Axes of the slice: x: 2, y: 2, z: 4, core: 2. Of those that a mesh axis runs over, the one named last changes fastest.
Arguments:
- spatial: bfloat16 [512, 32, 512], P(('cuts', 'coil', 'frame')), parts along dimension 0, may hold values from -6 to 6
- temporal: bfloat16 [32, 64], P(('cuts', 'frame')), parts along dimension 0, may hold values from -0.75 to 0.75
- kspace: bfloat16 [32, 32, 256, 512], P(('cuts', 'frame'), 'coil'), parts along dimension 0, may hold values from -2 to 2
- sampled: int32 [32, 256], P(('cuts', 'frame')), parts along dimension 0, may hold values 0 or 1
- sensitivity: bfloat16 [64, 256, 512], P(('cuts', 'coil')), parts along dimension 0, may hold values from -1 to 1
Outputs:
- spatial_grad: float32 [512, 32, 512], P(('cuts', 'coil', 'frame')), parts along dimension 0
- temporal_grad: float32 [32, 64], P(('cuts', 'frame')), parts along dimension 0
There are 2 independent parts, one for each index of `cuts`. A program takes and returns all parts, laid end to end along the dimension named above; each array names one. Nothing has to cross between parts.
All inputs are finite; a program needn't handle non-finite values. No bound on the sum of `sampled` on one device may be relied on, other than what follows from the above.
Results may differ from a plain program's by a relative error of at most 0.003.
Values may be sent and summed in bfloat16 or wider, within the bound.
No kernel may reach another device: no remote copies, remote signals or barrier semaphores. Data moves between devices by JAX's collectives and lax.ppermute only.
A program may use at most 128 MiB of HBM per device.

v0:
```python
import math
import jax
import jax.numpy as jnp
from jax import lax
from jax.sharding import PartitionSpec as P


def split_parts(values):
    half_width = values.shape[-1] // 2
    return (values[..., :half_width], values[..., half_width:])


def dft_block(length):
    index = jnp.arange(length, dtype=jnp.int32)
    angles = (index[:, None] * index[None, :] % length).astype(jnp.float32) * (
        2.0 * math.pi / length
    )
    norm_factor = 1.0 / math.sqrt(length)
    cosine = jnp.cos(angles) * norm_factor
    sine_part = -jnp.sin(angles) * norm_factor
    upper_rows = jnp.concatenate([cosine, sine_part], 1)
    lower_rows = jnp.concatenate([-sine_part, cosine], 1)
    return jnp.concatenate([upper_rows, lower_rows], 0).astype(jnp.bfloat16)


def to_image(temporal, spatial):
    temp_real, temp_imag = split_parts(temporal)
    spat_real, spat_imag = split_parts(spatial)
    image_real = jnp.einsum(
        "tr,xry->txy", temp_real, spat_real, preferred_element_type=jnp.float32
    ) - jnp.einsum("tr,xry->txy", temp_imag, spat_imag, preferred_element_type=jnp.float32)
    image_imag = jnp.einsum(
        "tr,xry->txy", temp_real, spat_imag, preferred_element_type=jnp.float32
    ) + jnp.einsum("tr,xry->txy", temp_imag, spat_real, preferred_element_type=jnp.float32)
    return jnp.concatenate([image_real, image_imag], -1).astype(jnp.bfloat16)


def factor_grad(temporal, grad_image):
    temp_real, temp_imag = split_parts(temporal)
    grad_real, grad_imag = split_parts(grad_image)
    spatial_real = jnp.einsum(
        "tr,txy->xry", temp_real, grad_real, preferred_element_type=jnp.float32
    ) + jnp.einsum("tr,txy->xry", temp_imag, grad_imag, preferred_element_type=jnp.float32)
    spatial_imag = jnp.einsum(
        "tr,txy->xry", temp_real, grad_imag, preferred_element_type=jnp.float32
    ) - jnp.einsum("tr,txy->xry", temp_imag, grad_real, preferred_element_type=jnp.float32)
    return jnp.concatenate([spatial_real, spatial_imag], -1)


def frame_grad(spatial, grad_image):
    spat_real, spat_imag = split_parts(spatial)
    grad_real, grad_imag = split_parts(grad_image)
    temporal_real = jnp.einsum(
        "xry,txy->tr", spat_real, grad_real, preferred_element_type=jnp.float32
    ) + jnp.einsum("xry,txy->tr", spat_imag, grad_imag, preferred_element_type=jnp.float32)
    temporal_imag = jnp.einsum(
        "xry,txy->tr", spat_real, grad_imag, preferred_element_type=jnp.float32
    ) - jnp.einsum("xry,txy->tr", spat_imag, grad_real, preferred_element_type=jnp.float32)
    return jnp.concatenate([temporal_real, temporal_imag], -1)


def coil_adjoint(image, measured, sampled_row, sensitivity, block):
    image_real, image_imag = split_parts(image.astype(jnp.float32))
    sens_real, sens_imag = split_parts(sensitivity.astype(jnp.float32))
    coil_real = sens_real * image_real[None] - sens_imag * image_imag[None]
    coil_imag = sens_real * image_imag[None] + sens_imag * image_real[None]
    coil_image = jnp.concatenate([coil_real, coil_imag], -1).astype(jnp.bfloat16)
    coil_count, row_count, full_width = coil_image.shape
    spectrum = jnp.dot(
        coil_image.reshape(coil_count * row_count, full_width),
        block,
        preferred_element_type=jnp.float32,
    ).reshape(coil_count, row_count, full_width)
    line_keep = jnp.concatenate([sampled_row, sampled_row]).astype(jnp.float32)
    misfit = (line_keep * (spectrum - measured.astype(jnp.float32))).astype(jnp.bfloat16)
    adjoint = jnp.dot(
        misfit.reshape(coil_count * row_count, full_width),
        block.T,
        preferred_element_type=jnp.float32,
    ).reshape(coil_count, row_count, full_width)
    back_real, back_imag = split_parts(adjoint)
    grad_real = jnp.sum(sens_real * back_real + sens_imag * back_imag, axis=0)
    grad_imag = jnp.sum(sens_real * back_imag - sens_imag * back_real, axis=0)
    return jnp.concatenate([grad_real, grad_imag], -1)


def on_device(spatial, temporal, kspace, sampled, sensitivity):
    block = dft_block(spatial.shape[2] // 2)
    temporal_all = lax.all_gather(temporal, "frame", axis=0, tiled=True)
    image_rows = to_image(temporal_all, spatial)
    image_half = lax.all_to_all(image_rows, "frame", split_axis=0, concat_axis=1, tiled=True)
    image_full = lax.all_gather(image_half, "coil", axis=1, tiled=True)
    coil_partial = lax.map(
        lambda frame_item: coil_adjoint(
            frame_item[0], frame_item[1], frame_item[2], sensitivity, block
        ),
        (image_full, kspace, sampled),
    )
    grad_half = lax.psum_scatter(coil_partial, "coil", scatter_dimension=1, tiled=True).astype(
        jnp.bfloat16
    )
    grad_rows = lax.all_to_all(grad_half, "frame", split_axis=1, concat_axis=0, tiled=True)
    spatial_grad = factor_grad(temporal_all, grad_rows)
    temporal_part = lax.psum_scatter(
        frame_grad(spatial, grad_rows), "frame", scatter_dimension=0, tiled=True
    )
    temporal_grad = lax.psum(temporal_part, "coil")
    return (spatial_grad, temporal_grad)


def solution(mesh):
    placed = (
        P(("cuts", "coil", "frame"), None, None),
        P(("cuts", "frame"), None),
        P(("cuts", "frame"), "coil", None, None),
        P(("cuts", "frame"), None),
        P(("cuts", "coil"), None, None),
    )
    return jax.shard_map(
        on_device,
        mesh=mesh,
        in_specs=placed,
        out_specs=(P(("cuts", "coil", "frame"), None, None), P(("cuts", "frame"), None)),
        check_vma=False,
    )
```

profile of v0, /device:TPU:0, one launch (start us, length us, event | category | flops | bytes accessed | tf_op | source)
XLA Modules:
  0.0 152.4 jit_solution(3036720703098302424)
XLA Ops:
  0.6 22.5 %all-gather = bf16[8,2,64]{2,1,0:T(2,128)(2,1)S(1)} all-gather(bf16[1,2,64]{2,1,0:T(2,128)(2,1)} %bitcast.83), channel_id=1, replica_groups=mesh['cuts'=2,'frame'=8,'coil'=2] {'frame'}, dimensions={0}, use_global_device_ids=true | all-gather | bytes 2304 | tf_op jit(solution)/shard_map/all_gather | solution.py:89
  23.1 1.1 fusion.41
  24.2 1.1 fusion.35
  25.3 1.2 fusion.22
  26.5 1.2 fusion.23
  27.7 0.8 copy.13
  28.6 3.4 %all-to-all-start = ((bf16[16,16,512]{2,1,0:T(8,128)(2,1)}), bf16[16,16,512]{2,1,0:T(8,128)(2,1)S(1)}, u32[]{:S(2)}, u32[]{:S(2)}) async-start(bf16[16,16,512]{2,1,0:T(8,128)(2,1)} %copy.13), calls=%async_computation | async-start | bytes 524288 | tf_op jit(solution)/shard_map/all_to_all | solution.py:91
  32.0 1.3 dynamic-slice
  33.9 1.0 fusion.32
  34.9 1.1 negate_convert_fusion
  36.0 0.8 maximum_maximum_fusion
  36.9 3.3 %all-to-all-done = bf16[16,16,512]{2,1,0:T(8,128)(2,1)S(1)} async-done(((bf16[16,16,512]{2,1,0:T(8,128)(2,1)}), bf16[16,16,512]{2,1,0:T(8,128)(2,1)S(1)}, u32[]{:S(2)}, u32[]{:S(2)}) %all-to-all-start) | async-done | bytes 262176 | tf_op jit(solution)/shard_map/all_to_all | solution.py:91
  40.2 2.2 %all_gather.7 = bf16[2,256,512]{2,1,0:T(8,128)(2,1)S(1)} all-gather(bf16[2,128,512]{2,1,0:T(8,128)(2,1)S(1)} %bitcast.70), channel_id=1, replica_groups=mesh['cuts'=2,'frame'=8,'coil'=2] {'coil'}, dimensions={1}, use_global_device_ids=true | all-gather | bytes 786432 | tf_op jit(solution)/shard_map/all_gather | solution.py:92
  42.4 62.9 %while.10 = (s32[]{:T(128)}, f32[2,256,512]{2,0,1:T(2,128)}, bf16[16,256,512]{2,1,0:T(8,128)(2,1)}, s32[2,256]{1,0:T(2,128)S(1)}, bf16[2,256,512]{2,1,0:T(8,128)...) while((s32[]{:T(128)}, f32[2,256,512]{2,0,1:T(2,128)}, ...), condition=%wide.region_3.4_spmd, body=%wide.region_0.3_spmd.sunk | while | flops 4330750976 | bytes 107749048 | solution.py:93
  42.5 3.4 %convert_element_type.64 = f32[16,256,512]{2,1,0:T(8,128)S(1)} convert(bf16[16,256,512]{2,1,0:T(8,128)(2,1)} %get-tuple-element.137) | non-fusion elementwise | flops 2097152 | bytes 12582912 | tf_op jit(solution)/shard_map/while/body/eval_jaxpr/convert_element_type | solution.py:64
  45.9 3.0 %subtract_convert_fusion.2 = (bf16[16,256,256]{2,1,0:T(8,128)(2,1)S(1)}, bf16[16,256,256]{2,1,0:T(8,128)(2,1)}) fusion(f32[16,256,512]{2,1,0:T(8,128)S(1)} %convert_element_type.64, f32[256,256]{1,0:T(8,128)S(1)} %get-tuple-element.111, f32[256,256]{1,0:T(8,128)S(1)} %get-tuple-element.112), kind=kLoop, calls=%fused_computation.13.clone.1 | loop fusion | flops 8388608 | bytes 13107200 | tf_op jit(solution)/shard_map/convert.2
  48.8 0.9 copy-done
  49.7 10.8 %fusion.65 = f32[16,256,512]{2,1,0:T(8,128)} fusion(bf16[2,16,256,512]{3,2,1,0:T(8,128)(2,1)} %get-tuple-element.141, s32[]{:T(128)} %get-tuple-element.126, f32[512]{0:T(512)S(1)} %add_convert_fusion.3, bf16[16,256,256]{2,1,0:T(8,128)(2,1)} %get-tuple-element.113, bf16[16,256,256]{2,1,0:T(8,128)(2,1)S(1)} %get-tuple-element.114, ...), kind=kOutput, calls=%fused_computation.3.clone.1 | convolution fusion | flops 4311744512 | bytes 17828352 | tf_op jit(solution)/shard_map/while/body/eval_jaxpr/dot_general | solution.py:76
  60.5 7.0 %add_reduce_fusion.2 = (f32[256,256]{1,0:T(8,128)S(1)}, f32[256,256]{1,0:T(8,128)S(1)}) fusion(f32[16,256,512]{2,1,0:T(8,128)} %fusion.65, f32[16,256,512]{2,1,0:T(8,128)} %copy-done), kind=kLoop, calls=%fused_computation.10.clone.1 | loop fusion | flops 8257536 | bytes 17301504 | tf_op jit(solution)/shard_map/while/body/eval_jaxpr/reduce_sum | solution.py:82
  67.6 0.5 copy.22
  68.2 4.7 %dynamic_update_slice.5 = f32[2,256,512]{2,0,1:T(2,128)S(1)} dynamic-update-slice(f32[2,256,512]{2,0,1:T(2,128)S(1)} %copy-done.2, f32[1,256,512]{2,0,1:T(1,128)S(1)} %copy.22, s32[]{:T(128)} %get-tuple-element.126, s32[]{:T(128)} %constant.31.clone.1..sunk, s32[]{:T(128)} %constant.31.clone.1..sunk) | dynamic-update-slice | bytes 1048580 | tf_op jit(solution)/shard_map/while/body/jit(dynamic_update_index_in_dim)/dynamic_update_slice | solution.py:93
  72.9 1.0 copy-done.3
  74.0 3.3 %convert_element_type.64 = f32[16,256,512]{2,1,0:T(8,128)S(1)} convert(bf16[16,256,512]{2,1,0:T(8,128)(2,1)} %get-tuple-element.137) | non-fusion elementwise | flops 2097152 | bytes 12582912 | tf_op jit(solution)/shard_map/while/body/eval_jaxpr/convert_element_type | solution.py:64
  77.3 3.0 %subtract_convert_fusion.2 = (bf16[16,256,256]{2,1,0:T(8,128)(2,1)S(1)}, bf16[16,256,256]{2,1,0:T(8,128)(2,1)}) fusion(f32[16,256,512]{2,1,0:T(8,128)S(1)} %convert_element_type.64, f32[256,256]{1,0:T(8,128)S(1)} %get-tuple-element.111, f32[256,256]{1,0:T(8,128)S(1)} %get-tuple-element.112), kind=kLoop, calls=%fused_computation.13.clone.1 | loop fusion | flops 8388608 | bytes 13107200 | tf_op jit(solution)/shard_map/convert.2
  80.3 0.9 copy-done
  81.2 10.8 %fusion.65 = f32[16,256,512]{2,1,0:T(8,128)} fusion(bf16[2,16,256,512]{3,2,1,0:T(8,128)(2,1)} %get-tuple-element.141, s32[]{:T(128)} %get-tuple-element.126, f32[512]{0:T(512)S(1)} %add_convert_fusion.3, bf16[16,256,256]{2,1,0:T(8,128)(2,1)} %get-tuple-element.113, bf16[16,256,256]{2,1,0:T(8,128)(2,1)S(1)} %get-tuple-element.114, ...), kind=kOutput, calls=%fused_computation.3.clone.1 | convolution fusion | flops 4311744512 | bytes 17828352 | tf_op jit(solution)/shard_map/while/body/eval_jaxpr/dot_general | solution.py:76
  91.9 7.0 %add_reduce_fusion.2 = (f32[256,256]{1,0:T(8,128)S(1)}, f32[256,256]{1,0:T(8,128)S(1)}) fusion(f32[16,256,512]{2,1,0:T(8,128)} %fusion.65, f32[16,256,512]{2,1,0:T(8,128)} %copy-done), kind=kLoop, calls=%fused_computation.10.clone.1 | loop fusion | flops 8257536 | bytes 17301504 | tf_op jit(solution)/shard_map/while/body/eval_jaxpr/reduce_sum | solution.py:82
  99.0 0.5 copy.22
  99.6 4.7 %dynamic_update_slice.5 = f32[2,256,512]{2,0,1:T(2,128)S(1)} dynamic-update-slice(f32[2,256,512]{2,0,1:T(2,128)S(1)} %copy-done.2, f32[1,256,512]{2,0,1:T(1,128)S(1)} %copy.22, s32[]{:T(128)} %get-tuple-element.126, s32[]{:T(128)} %constant.31.clone.1..sunk, s32[]{:T(128)} %constant.31.clone.1..sunk) | dynamic-update-slice | bytes 1048580 | tf_op jit(solution)/shard_map/while/body/jit(dynamic_update_index_in_dim)/dynamic_update_slice | solution.py:93
  104.3 1.0 copy-done.3
  105.3 6.9 %all-reduce.3 = bf16[2,256,512]{2,0,1:T(2,128)(2,1)S(1)} all-reduce(f32[2,256,512]{2,0,1:T(2,128)} %get-tuple-element.39), channel_id=2, replica_groups=mesh['cuts'=2,'frame'=8,'coil'=2] {'coil'}, use_global_device_ids=true, to_apply=%region_4.5.clone | all-reduce | flops 262144 | bytes 1572864
  112.2 0.9 dynamic-slice_convert_fusion
  113.1 3.4 %all-to-all-start.1 = ((bf16[2,128,512]{2,0,1:T(2,128)(2,1)}), bf16[2,128,512]{2,0,1:T(2,128)(2,1)S(1)}, u32[]{:S(2)}, u32[]{:S(2)}) async-start(bf16[2,128,512]{2,0,1:T(2,128)(2,1)} %dynamic-slice_convert_fusion), calls=%async_computation.1 | async-start | bytes 524288 | tf_op jit(solution)/shard_map/all_to_all | solution.py:102
  116.5 0.6 dynamic-slice.2
  117.7 8.4 %all-to-all-done.1 = bf16[2,128,512]{2,0,1:T(2,128)(2,1)S(1)} async-done(((bf16[2,128,512]{2,0,1:T(2,128)(2,1)}), bf16[2,128,512]{2,0,1:T(2,128)(2,1)S(1)}, u32[]{:S(2)}, u32[]{:S(2)}) %all-to-all-start.1) | async-done | bytes 262176 | tf_op jit(solution)/shard_map/all_to_all | solution.py:102
  126.2 0.2 copy.20
  126.4 0.1 all_to_all.33
  126.5 0.2 convolution_bitcast_fusion.3
  126.7 0.2 convolution_bitcast_fusion.1
  126.9 0.3 fusion.51
  127.2 0.3 fusion.45
  127.4 0.2 fusion.25
  127.6 0.2 fusion.24
  127.9 19.6 %all-reduce.1 = f32[16,64]{1,0:T(8,128)S(1)} all-reduce(f32[16,64]{1,0:T(8,128)S(1)} %pad_maximum_fusion.2), channel_id=3, replica_groups=mesh['cuts'=2,'frame'=8,'coil'=2] {'frame'}, use_global_device_ids=true, to_apply=%region_5.6.clone | all-reduce | flops 1024 | bytes 8192
  147.6 3.0 %psum.7 = f32[2,64]{1,0:T(2,128)} all-reduce(f32[2,64]{1,0:T(2,128)S(1)} %constant_dynamic-slice_fusion.1), channel_id=1, replica_groups=mesh['cuts'=2,'frame'=8,'coil'=2] {'coil'}, use_global_device_ids=true, to_apply=%region_6.7 | all-reduce | flops 128 | bytes 1024 | tf_op jit(solution)/shard_map/psum | solution.py:107
  150.6 0.3 fusion.21
  150.9 0.3 fusion.20
  151.3 1.1 pad_maximum_fusion
  (29 shorter events, 0.5 us)
Async XLA Ops:
  0.6 41.7 %copy-start.4 = (s32[2,256]{1,0:T(2,128)S(1)}, s32[2,256]{1,0:T(2,128)}, u32[]{:S(2)}) copy-start(s32[2,256]{1,0:T(2,128)} %param.10) | copy-start | bytes 6148
  28.6 11.6 %all-to-all-start = ((bf16[16,16,512]{2,1,0:T(8,128)(2,1)}), bf16[16,16,512]{2,1,0:T(8,128)(2,1)S(1)}, u32[]{:S(2)}, u32[]{:S(2)}) async-start(bf16[16,16,512]{2,1,0:T(8,128)(2,1)} %copy.13), calls=%async_computation | async-start | bytes 524288 | tf_op jit(solution)/shard_map/all_to_all | solution.py:91
  42.4 74.1 %copy-start.5 = (u32[32]{0:T(128)S(1)}, u32[32]{0:T(128)}, u32[]{:S(2)}) copy-start(u32[32]{0:T(128)} %constant.47) | copy-start | bytes 388
  42.4 84.1 %copy-start.1 = (bf16[16,32,512]{2,1,0:T(8,128)(2,1)S(1)}, bf16[16,32,512]{2,1,0:T(8,128)(2,1)}, u32[]{:S(2)}) copy-start(bf16[16,32,512]{2,1,0:T(8,128)(2,1)} %param.7) | copy-start | bytes 1572868
  45.9 3.8 %copy-start = (f32[16,256,512]{2,1,0:T(8,128)}, f32[16,256,512]{2,1,0:T(8,128)S(1)}, u32[]{:S(2)}) copy-start(f32[16,256,512]{2,1,0:T(8,128)S(1)} %convert_element_type.64) | copy-start | bytes 25165828 | tf_op jit(solution)/shard_map/while
  60.5 7.6 %copy-start.2 = (f32[2,256,512]{2,0,1:T(2,128)S(1)}, f32[2,256,512]{2,0,1:T(2,128)}, u32[]{:S(2)}) copy-start(f32[2,256,512]{2,0,1:T(2,128)} %get-tuple-element.127) | copy-start | bytes 3145732 | tf_op jit(solution)/shard_map/while
  72.9 1.0 copy-start.3
  77.3 3.8 %copy-start = (f32[16,256,512]{2,1,0:T(8,128)}, f32[16,256,512]{2,1,0:T(8,128)S(1)}, u32[]{:S(2)}) copy-start(f32[16,256,512]{2,1,0:T(8,128)S(1)} %convert_element_type.64) | copy-start | bytes 25165828 | tf_op jit(solution)/shard_map/while
  91.9 7.6 %copy-start.2 = (f32[2,256,512]{2,0,1:T(2,128)S(1)}, f32[2,256,512]{2,0,1:T(2,128)}, u32[]{:S(2)}) copy-start(f32[2,256,512]{2,0,1:T(2,128)} %get-tuple-element.127) | copy-start | bytes 3145732 | tf_op jit(solution)/shard_map/while
  104.3 1.0 copy-start.3
  113.1 13.1 %all-to-all-start.1 = ((bf16[2,128,512]{2,0,1:T(2,128)(2,1)}), bf16[2,128,512]{2,0,1:T(2,128)(2,1)S(1)}, u32[]{:S(2)}, u32[]{:S(2)}) async-start(bf16[2,128,512]{2,0,1:T(2,128)(2,1)} %dynamic-slice_convert_fusion), calls=%async_computation.1 | async-start | bytes 524288 | tf_op jit(solution)/shard_map/all_to_all | solution.py:102
where the time goes:
time: 153 us; the launch traced here: 152 us
  blocking collectives  54.2 us (35%)
  other arithmetic  31 us (20%)
  matrix products  28.1 us (18%)
  local copies, waits for them, and re-layouts  18.2 us (12%)
  waiting for transfers between devices  11.7 us (8%)
  starting transfers between devices  6.82 us (4%)
  between operations  2.1 us (1%)
    unnamed x2, blocking collectives  26.5 us
    all_gather x1, blocking collectives, on_device(): temporal_all = lax.all_gather(temporal, 'frame', axis=0, tiled=True)  22.5 us
    dot_general x2, matrix products, coil_adjoint(): jnp.dot(misfit.reshape(coil_count * row_count, full_width), block.T, pref...  21.6 us
    reduce_sum x2, other arithmetic, coil_adjoint(): grad_real = jnp.sum(sens_real * back_real + sens_imag * back_imag, axis=0)  14 us
    dynamic_update_slice x4, local copies, waits for them, and re-layouts, on_device(): lax.map(lambda frame_item: coil_adjoint(frame_item[0], frame_item[1], fra...  10.5 us
    all_to_all x1, waiting for transfers between devices, on_device(): lax.all_to_all(grad_half, 'frame', split_axis=1, concat_axis=0, tiled=True)  8.41 us
    another operation x4, other arithmetic  8 us
    convert_element_type x2, other arithmetic, coil_adjoint(): sens_real, sens_imag = split_parts(sensitivity.astype(jnp.float32))  6.72 us
  transfers between devices with their start and end apart: 2, of which 2 were waited for; matrix products, arithmetic and copies ran while one was open for 3% of the time, Pallas kernels for 0%

commit v1 on v0

--- a/solution.py
+++ b/solution.py
@@ -3,6 +3,23 @@
 import jax.numpy as jnp
 from jax import lax
 from jax.sharding import PartitionSpec as P
+
+
+def joined_along(blocks, dim):
+    shape = list(blocks.shape[1:])
+    shape[dim] *= blocks.shape[0]
+    return jnp.moveaxis(blocks, 0, dim).reshape(shape)
+
+
+def doubled(x, axis):
+    size, position = (lax.axis_size(axis), lax.axis_index(axis))
+    blocks, bit = (x[None], 1)
+    while bit < size:
+        other = lax.ppermute(blocks, axis, [(i, i ^ bit) for i in range(size)])
+        low = position & bit == 0
+        blocks = jnp.concatenate([jnp.where(low, blocks, other), jnp.where(low, other, blocks)])
+        bit *= 2
+    return blocks
 
 
 def split_parts(values):
@@ -86,7 +103,7 @@
 
 def on_device(spatial, temporal, kspace, sampled, sensitivity):
     block = dft_block(spatial.shape[2] // 2)
-    temporal_all = lax.all_gather(temporal, "frame", axis=0, tiled=True)
+    temporal_all = joined_along(doubled(temporal, "frame"), 0)
     image_rows = to_image(temporal_all, spatial)
     image_half = lax.all_to_all(image_rows, "frame", split_axis=0, concat_axis=1, tiled=True)
     image_full = lax.all_gather(image_half, "coil", axis=1, tiled=True)

time: 153 us -> 147 us (0.961)
  blocking collectives: 54.2 us -> 31.7 us
  starting transfers between devices: 6.82 us -> 17.9 us
  waiting for transfers between devices: 11.7 us -> 16.6 us
    all_gather x1 -> x0, blocking collectives: 22.5 us -> none  [on_device(): temporal_all = lax.all_gather(temporal, 'frame', axis=0, tiled=True)]
    ppermute x0 -> x3, starting transfers between devices: none -> 8.3 us  [doubled(): other = lax.ppermute(blocks, axis, [(i, i ^ bit) for i in range(size)])]
    ppermute x0 -> x3, waiting for transfers between devices: none -> 4.8 us  [doubled(): other = lax.ppermute(blocks, axis, [(i, i ^ bit) for i in range(size)])]
    all_to_all x1, starting transfers between devices: 3.41 us -> 6.16 us  [on_device(): lax.all_to_all(image_rows, 'frame', split_axis=0, concat_axis=1, tiled=True)]
  transfers between devices with their start and end apart: 2 -> 5, of which waited for: 2 -> 5; matrix products, arithmetic and copies ran while one was open for 3% -> 3% of each run, Pallas kernels for 0% -> 0%
where the time goes in v1:
time: 147 us
  other arithmetic  31.7 us (22%)
  blocking collectives  31.7 us (22%)
  matrix products  28.1 us (19%)
  local copies, waits for them, and re-layouts  18.3 us (12%)
  starting transfers between devices  17.9 us (12%)
  waiting for transfers between devices  16.6 us (11%)
  between operations  2.1 us (1%)
    unnamed x2, blocking collectives  26.5 us
    dot_general x2, matrix products, coil_adjoint(): jnp.dot(misfit.reshape(coil_count * row_count, full_width), block.T, pref...  21.6 us
    reduce_sum x2, other arithmetic, coil_adjoint(): grad_real = jnp.sum(sens_real * back_real + sens_imag * back_imag, axis=0)  14 us
    dynamic_update_slice x4, local copies, waits for them, and re-layouts, on_device(): lax.map(lambda frame_item: coil_adjoint(frame_item[0], frame_item[1], fra...  10.5 us
    all_to_all x1, waiting for transfers between devices, on_device(): lax.all_to_all(grad_half, 'frame', split_axis=1, concat_axis=0, tiled=True)  8.41 us
    ppermute x3, starting transfers between devices, doubled(): other = lax.ppermute(blocks, axis, [(i, i ^ bit) for i in range(size)])  8.3 us
    another operation x4, other arithmetic  7.99 us
    convert_element_type x2, other arithmetic, coil_adjoint(): sens_real, sens_imag = split_parts(sensitivity.astype(jnp.float32))  6.72 us
  transfers between devices with their start and end apart: 5, of which 5 were waited for; matrix products, arithmetic and copies ran while one was open for 3% of the time, Pallas kernels for 0%

profile of v1, /device:TPU:0, one launch (start us, length us, event | category | flops | bytes accessed | tf_op | source)
XLA Modules:
  0.0 146.6 jit_solution(997852255398467686)
XLA Ops:
  0.6 3.1 %collective-permute-start = (bf16[1,2,64]{2,1,0:T(2,128)(2,1)}, bf16[1,2,64]{2,1,0:T(2,128)(2,1)S(1)}, u32[]{:S(2)}, u32[]{:S(2)}) collective-permute-start(bf16[1,2,64]{2,1,0:T(2,128)(2,1)} %bitcast.85), channel_id=1, source_target_pairs={{0,2},{2,0},{4,6},{6,4},{8,10},{10,8},{12,14},{14,12},{1,3},{3,1},... | collective-permute-start | bytes 776 | tf_op jit(solution)/shard_map/ppermute | solution.py:18
  3.7 1.7 %collective-permute-done = bf16[1,2,64]{2,1,0:T(2,128)(2,1)S(1)} collective-permute-done((bf16[1,2,64]{2,1,0:T(2,128)(2,1)}, bf16[1,2,64]{2,1,0:T(2,128)(2,1)S(1)}, u32[]{:S(2)}, u32[]{:S(2)}) %collective-permute-start) | collective-permute-done | bytes 288 | tf_op jit(solution)/shard_map/ppermute | solution.py:18
  5.4 0.7 broadcast_select_fusion.5
  6.1 2.1 %collective-permute-start.1 = (bf16[2,2,64]{2,1,0:T(2,128)(2,1)S(1)}, bf16[2,2,64]{2,1,0:T(2,128)(2,1)S(1)}, u32[]{:S(2)}, u32[]{:S(2)}) collective-permute-start(bf16[2,2,64]{2,1,0:T(2,128)(2,1)S(1)} %pad_maximum_fusion.5), channel_id=1, source_target_pairs={{0,4},{2,6},{4,0},{6,2},{8,12},{10,14},{12,8},{14,10},{1,5},{3,7},... | collective-permute-start | bytes 1544 | tf_op jit(solution)/shard_map/ppermute | solution.py:18
  8.2 1.6 %collective-permute-done.1 = bf16[2,2,64]{2,1,0:T(2,128)(2,1)S(1)} collective-permute-done((bf16[2,2,64]{2,1,0:T(2,128)(2,1)S(1)}, bf16[2,2,64]{2,1,0:T(2,128)(2,1)S(1)}, u32[]{:S(2)}, u32[]{:S(2)}) %collective-permute-start.1) | collective-permute-done | bytes 544 | tf_op jit(solution)/shard_map/ppermute | solution.py:18
  9.8 3.1 %collective-permute-start.2 = (bf16[4,2,64]{2,1,0:T(2,128)(2,1)S(1)}, bf16[4,2,64]{2,1,0:T(2,128)(2,1)S(1)}, u32[]{:S(2)}, u32[]{:S(2)}) collective-permute-start(bf16[4,2,64]{2,1,0:T(2,128)(2,1)S(1)} %pad_maximum_fusion.4), channel_id=1, source_target_pairs={{0,8},{2,10},{4,12},{6,14},{8,0},{10,2},{12,4},{14,6},{1,9},{3,11}... | collective-permute-start | bytes 3080 | tf_op jit(solution)/shard_map/ppermute | solution.py:18
  12.9 1.6 %collective-permute-done.2 = bf16[4,2,64]{2,1,0:T(2,128)(2,1)S(1)} collective-permute-done((bf16[4,2,64]{2,1,0:T(2,128)(2,1)S(1)}, bf16[4,2,64]{2,1,0:T(2,128)(2,1)S(1)}, u32[]{:S(2)}, u32[]{:S(2)}) %collective-permute-start.2) | collective-permute-done | bytes 1056 | tf_op jit(solution)/shard_map/ppermute | solution.py:18
  14.5 1.1 fusion.41
  15.6 1.1 fusion.35
  16.7 1.2 fusion.22
  17.9 1.2 fusion.23
  19.1 0.9 copy.13
  20.0 6.2 %all-to-all-start = ((bf16[16,16,512]{2,1,0:T(8,128)(2,1)}), bf16[16,16,512]{2,1,0:T(8,128)(2,1)S(1)}, u32[]{:S(2)}, u32[]{:S(2)}) async-start(bf16[16,16,512]{2,1,0:T(8,128)(2,1)} %copy.13), calls=%async_computation | async-start | bytes 524288 | tf_op jit(solution)/shard_map/all_to_all | solution.py:108
  26.1 1.3 dynamic-slice
  28.0 1.0 fusion.32
  29.0 1.1 negate_convert_fusion
  30.1 0.8 maximum_maximum_fusion
  31.0 3.4 %all-to-all-done = bf16[16,16,512]{2,1,0:T(8,128)(2,1)S(1)} async-done(((bf16[16,16,512]{2,1,0:T(8,128)(2,1)}), bf16[16,16,512]{2,1,0:T(8,128)(2,1)S(1)}, u32[]{:S(2)}, u32[]{:S(2)}) %all-to-all-start) | async-done | bytes 262176 | tf_op jit(solution)/shard_map/all_to_all | solution.py:108
  34.4 2.2 %all_gather.3 = bf16[2,256,512]{2,1,0:T(8,128)(2,1)S(1)} all-gather(bf16[2,128,512]{2,1,0:T(8,128)(2,1)S(1)} %bitcast.72), channel_id=1, replica_groups=mesh['cuts'=2,'frame'=8,'coil'=2] {'coil'}, dimensions={1}, use_global_device_ids=true | all-gather | bytes 786432 | tf_op jit(solution)/shard_map/all_gather | solution.py:109
  36.6 63.0 %while.10 = (s32[]{:T(128)}, f32[2,256,512]{2,0,1:T(2,128)}, bf16[16,256,512]{2,1,0:T(8,128)(2,1)}, s32[2,256]{1,0:T(2,128)S(1)}, bf16[2,256,512]{2,1,0:T(8,128)...) while((s32[]{:T(128)}, f32[2,256,512]{2,0,1:T(2,128)}, ...), condition=%wide.region_3.4_spmd, body=%wide.region_0.3_spmd.sunk | while | flops 4330750976 | bytes 107749048 | solution.py:110
  36.7 3.4 %convert_element_type.64 = f32[16,256,512]{2,1,0:T(8,128)S(1)} convert(bf16[16,256,512]{2,1,0:T(8,128)(2,1)} %get-tuple-element.143) | non-fusion elementwise | flops 2097152 | bytes 12582912 | tf_op jit(solution)/shard_map/while/body/eval_jaxpr/convert_element_type | solution.py:81
  40.1 2.9 %subtract_convert_fusion.2 = (bf16[16,256,256]{2,1,0:T(8,128)(2,1)S(1)}, bf16[16,256,256]{2,1,0:T(8,128)(2,1)}) fusion(f32[16,256,512]{2,1,0:T(8,128)S(1)} %convert_element_type.64, f32[256,256]{1,0:T(8,128)S(1)} %get-tuple-element.117, f32[256,256]{1,0:T(8,128)S(1)} %get-tuple-element.118), kind=kLoop, calls=%fused_computation.13.clone.1 | loop fusion | flops 8388608 | bytes 13107200 | tf_op jit(solution)/shard_map/convert.2
  43.0 0.9 copy-done
  43.9 10.8 %fusion.65 = f32[16,256,512]{2,1,0:T(8,128)} fusion(bf16[2,16,256,512]{3,2,1,0:T(8,128)(2,1)} %get-tuple-element.147, s32[]{:T(128)} %get-tuple-element.132, f32[512]{0:T(512)S(1)} %add_convert_fusion.3, bf16[16,256,256]{2,1,0:T(8,128)(2,1)} %get-tuple-element.119, bf16[16,256,256]{2,1,0:T(8,128)(2,1)S(1)} %get-tuple-element.120, ...), kind=kOutput, calls=%fused_computation.3.clone.1 | convolution fusion | flops 4311744512 | bytes 17828352 | tf_op jit(solution)/shard_map/while/body/eval_jaxpr/dot_general | solution.py:93
  54.8 7.0 %add_reduce_fusion.2 = (f32[256,256]{1,0:T(8,128)S(1)}, f32[256,256]{1,0:T(8,128)S(1)}) fusion(f32[16,256,512]{2,1,0:T(8,128)} %fusion.65, f32[16,256,512]{2,1,0:T(8,128)} %copy-done), kind=kLoop, calls=%fused_computation.10.clone.1 | loop fusion | flops 8257536 | bytes 17301504 | tf_op jit(solution)/shard_map/while/body/eval_jaxpr/reduce_sum | solution.py:99
  61.8 0.5 copy.22
  62.4 4.7 %dynamic_update_slice.5 = f32[2,256,512]{2,0,1:T(2,128)S(1)} dynamic-update-slice(f32[2,256,512]{2,0,1:T(2,128)S(1)} %copy-done.2, f32[1,256,512]{2,0,1:T(1,128)S(1)} %copy.22, s32[]{:T(128)} %get-tuple-element.132, s32[]{:T(128)} %constant.24.clone.1..sunk, s32[]{:T(128)} %constant.24.clone.1..sunk) | dynamic-update-slice | bytes 1048580 | tf_op jit(solution)/shard_map/while/body/jit(dynamic_update_index_in_dim)/dynamic_update_slice | solution.py:110
  67.1 1.0 copy-done.3
  68.2 3.3 %convert_element_type.64 = f32[16,256,512]{2,1,0:T(8,128)S(1)} convert(bf16[16,256,512]{2,1,0:T(8,128)(2,1)} %get-tuple-element.143) | non-fusion elementwise | flops 2097152 | bytes 12582912 | tf_op jit(solution)/shard_map/while/body/eval_jaxpr/convert_element_type | solution.py:81
  71.5 2.9 %subtract_convert_fusion.2 = (bf16[16,256,256]{2,1,0:T(8,128)(2,1)S(1)}, bf16[16,256,256]{2,1,0:T(8,128)(2,1)}) fusion(f32[16,256,512]{2,1,0:T(8,128)S(1)} %convert_element_type.64, f32[256,256]{1,0:T(8,128)S(1)} %get-tuple-element.117, f32[256,256]{1,0:T(8,128)S(1)} %get-tuple-element.118), kind=kLoop, calls=%fused_computation.13.clone.1 | loop fusion | flops 8388608 | bytes 13107200 | tf_op jit(solution)/shard_map/convert.2
  74.5 0.9 copy-done
  75.4 10.8 %fusion.65 = f32[16,256,512]{2,1,0:T(8,128)} fusion(bf16[2,16,256,512]{3,2,1,0:T(8,128)(2,1)} %get-tuple-element.147, s32[]{:T(128)} %get-tuple-element.132, f32[512]{0:T(512)S(1)} %add_convert_fusion.3, bf16[16,256,256]{2,1,0:T(8,128)(2,1)} %get-tuple-element.119, bf16[16,256,256]{2,1,0:T(8,128)(2,1)S(1)} %get-tuple-element.120, ...), kind=kOutput, calls=%fused_computation.3.clone.1 | convolution fusion | flops 4311744512 | bytes 17828352 | tf_op jit(solution)/shard_map/while/body/eval_jaxpr/dot_general | solution.py:93
  86.2 7.0 %add_reduce_fusion.2 = (f32[256,256]{1,0:T(8,128)S(1)}, f32[256,256]{1,0:T(8,128)S(1)}) fusion(f32[16,256,512]{2,1,0:T(8,128)} %fusion.65, f32[16,256,512]{2,1,0:T(8,128)} %copy-done), kind=kLoop, calls=%fused_computation.10.clone.1 | loop fusion | flops 8257536 | bytes 17301504 | tf_op jit(solution)/shard_map/while/body/eval_jaxpr/reduce_sum | solution.py:99
  93.3 0.5 copy.22
  93.8 4.7 %dynamic_update_slice.5 = f32[2,256,512]{2,0,1:T(2,128)S(1)} dynamic-update-slice(f32[2,256,512]{2,0,1:T(2,128)S(1)} %copy-done.2, f32[1,256,512]{2,0,1:T(1,128)S(1)} %copy.22, s32[]{:T(128)} %get-tuple-element.132, s32[]{:T(128)} %constant.24.clone.1..sunk, s32[]{:T(128)} %constant.24.clone.1..sunk) | dynamic-update-slice | bytes 1048580 | tf_op jit(solution)/shard_map/while/body/jit(dynamic_update_index_in_dim)/dynamic_update_slice | solution.py:110
  98.6 1.0 copy-done.3
  99.5 6.9 %all-reduce.3 = bf16[2,256,512]{2,0,1:T(2,128)(2,1)S(1)} all-reduce(f32[2,256,512]{2,0,1:T(2,128)} %get-tuple-element.39), channel_id=2, replica_groups=mesh['cuts'=2,'frame'=8,'coil'=2] {'coil'}, use_global_device_ids=true, to_apply=%region_4.5.clone | all-reduce | flops 262144 | bytes 1572864
  106.4 0.9 dynamic-slice_convert_fusion
  107.3 3.4 %all-to-all-start.1 = ((bf16[2,128,512]{2,0,1:T(2,128)(2,1)}), bf16[2,128,512]{2,0,1:T(2,128)(2,1)S(1)}, u32[]{:S(2)}, u32[]{:S(2)}) async-start(bf16[2,128,512]{2,0,1:T(2,128)(2,1)} %dynamic-slice_convert_fusion), calls=%async_computation.1 | async-start | bytes 524288 | tf_op jit(solution)/shard_map/all_to_all | solution.py:119
  110.8 0.6 dynamic-slice.2
  112.0 8.4 %all-to-all-done.1 = bf16[2,128,512]{2,0,1:T(2,128)(2,1)S(1)} async-done(((bf16[2,128,512]{2,0,1:T(2,128)(2,1)}), bf16[2,128,512]{2,0,1:T(2,128)(2,1)S(1)}, u32[]{:S(2)}, u32[]{:S(2)}) %all-to-all-start.1) | async-done | bytes 262176 | tf_op jit(solution)/shard_map/all_to_all | solution.py:119
  121.1 0.3 fusion.51
  121.4 0.3 fusion.45
  122.1 19.6 %all-reduce.1 = f32[16,64]{1,0:T(8,128)S(1)} all-reduce(f32[16,64]{1,0:T(8,128)S(1)} %pad_maximum_fusion.2), channel_id=3, replica_groups=mesh['cuts'=2,'frame'=8,'coil'=2] {'frame'}, use_global_device_ids=true, to_apply=%region_5.6.clone | all-reduce | flops 1024 | bytes 8192
  141.8 3.0 %psum.7 = f32[2,64]{1,0:T(2,128)} all-reduce(f32[2,64]{1,0:T(2,128)S(1)} %constant_dynamic-slice_fusion.1), channel_id=1, replica_groups=mesh['cuts'=2,'frame'=8,'coil'=2] {'coil'}, use_global_device_ids=true, to_apply=%region_6.7 | all-reduce | flops 128 | bytes 1024 | tf_op jit(solution)/shard_map/psum | solution.py:124
  144.8 0.3 fusion.21
  145.2 0.3 fusion.20
  145.5 1.1 pad_maximum_fusion
  (40 shorter events, 1.6 us)
Async XLA Ops:
  0.6 35.9 %copy-start.4 = (s32[2,256]{1,0:T(2,128)S(1)}, s32[2,256]{1,0:T(2,128)}, u32[]{:S(2)}) copy-start(s32[2,256]{1,0:T(2,128)} %param.10) | copy-start | bytes 6148
  0.6 4.7 %collective-permute-start = (bf16[1,2,64]{2,1,0:T(2,128)(2,1)}, bf16[1,2,64]{2,1,0:T(2,128)(2,1)S(1)}, u32[]{:S(2)}, u32[]{:S(2)}) collective-permute-start(bf16[1,2,64]{2,1,0:T(2,128)(2,1)} %bitcast.85), channel_id=1, source_target_pairs={{0,2},{2,0},{4,6},{6,4},{8,10},{10,8},{12,14},{14,12},{1,3},{3,1},... | collective-permute-start | bytes 776 | tf_op jit(solution)/shard_map/ppermute | solution.py:18
  6.1 3.7 %collective-permute-start.1 = (bf16[2,2,64]{2,1,0:T(2,128)(2,1)S(1)}, bf16[2,2,64]{2,1,0:T(2,128)(2,1)S(1)}, u32[]{:S(2)}, u32[]{:S(2)}) collective-permute-start(bf16[2,2,64]{2,1,0:T(2,128)(2,1)S(1)} %pad_maximum_fusion.5), channel_id=1, source_target_pairs={{0,4},{2,6},{4,0},{6,2},{8,12},{10,14},{12,8},{14,10},{1,5},{3,7},... | collective-permute-start | bytes 1544 | tf_op jit(solution)/shard_map/ppermute | solution.py:18
  9.8 4.7 %collective-permute-start.2 = (bf16[4,2,64]{2,1,0:T(2,128)(2,1)S(1)}, bf16[4,2,64]{2,1,0:T(2,128)(2,1)S(1)}, u32[]{:S(2)}, u32[]{:S(2)}) collective-permute-start(bf16[4,2,64]{2,1,0:T(2,128)(2,1)S(1)} %pad_maximum_fusion.4), channel_id=1, source_target_pairs={{0,8},{2,10},{4,12},{6,14},{8,0},{10,2},{12,4},{14,6},{1,9},{3,11}... | collective-permute-start | bytes 3080 | tf_op jit(solution)/shard_map/ppermute | solution.py:18
  20.0 14.4 %all-to-all-start = ((bf16[16,16,512]{2,1,0:T(8,128)(2,1)}), bf16[16,16,512]{2,1,0:T(8,128)(2,1)S(1)}, u32[]{:S(2)}, u32[]{:S(2)}) async-start(bf16[16,16,512]{2,1,0:T(8,128)(2,1)} %copy.13), calls=%async_computation | async-start | bytes 524288 | tf_op jit(solution)/shard_map/all_to_all | solution.py:108
  36.6 74.2 %copy-start.5 = (u32[32]{0:T(128)S(1)}, u32[32]{0:T(128)}, u32[]{:S(2)}) copy-start(u32[32]{0:T(128)} %constant.59) | copy-start | bytes 388
  36.6 84.2 %copy-start.1 = (bf16[16,32,512]{2,1,0:T(8,128)(2,1)S(1)}, bf16[16,32,512]{2,1,0:T(8,128)(2,1)}, u32[]{:S(2)}) copy-start(bf16[16,32,512]{2,1,0:T(8,128)(2,1)} %param.7) | copy-start | bytes 1572868
  40.1 3.9 %copy-start = (f32[16,256,512]{2,1,0:T(8,128)}, f32[16,256,512]{2,1,0:T(8,128)S(1)}, u32[]{:S(2)}) copy-start(f32[16,256,512]{2,1,0:T(8,128)S(1)} %convert_element_type.64) | copy-start | bytes 25165828 | tf_op jit(solution)/shard_map/while
  54.8 7.6 %copy-start.2 = (f32[2,256,512]{2,0,1:T(2,128)S(1)}, f32[2,256,512]{2,0,1:T(2,128)}, u32[]{:S(2)}) copy-start(f32[2,256,512]{2,0,1:T(2,128)} %get-tuple-element.133) | copy-start | bytes 3145732 | tf_op jit(solution)/shard_map/while
  67.1 1.0 copy-start.3
  71.5 3.9 %copy-start = (f32[16,256,512]{2,1,0:T(8,128)}, f32[16,256,512]{2,1,0:T(8,128)S(1)}, u32[]{:S(2)}) copy-start(f32[16,256,512]{2,1,0:T(8,128)S(1)} %convert_element_type.64) | copy-start | bytes 25165828 | tf_op jit(solution)/shard_map/while
  86.2 7.6 %copy-start.2 = (f32[2,256,512]{2,0,1:T(2,128)S(1)}, f32[2,256,512]{2,0,1:T(2,128)}, u32[]{:S(2)}) copy-start(f32[2,256,512]{2,0,1:T(2,128)} %get-tuple-element.133) | copy-start | bytes 3145732 | tf_op jit(solution)/shard_map/while
  98.6 1.0 copy-start.3
  107.3 13.1 %all-to-all-start.1 = ((bf16[2,128,512]{2,0,1:T(2,128)(2,1)}), bf16[2,128,512]{2,0,1:T(2,128)(2,1)S(1)}, u32[]{:S(2)}, u32[]{:S(2)}) async-start(bf16[2,128,512]{2,0,1:T(2,128)(2,1)} %dynamic-slice_convert_fusion), calls=%async_computation.1 | async-start | bytes 524288 | tf_op jit(solution)/shard_map/all_to_all | solution.py:119
